TPU v7x, 512 devices: a whole 4x8x8 slice. The times are simulated.
512 devices in a mesh: dp: 2 (over core), ctx: 64 (over z, y), head: 4 (over x).
Axes of the slice: x: 4, y: 8, z: 8, core: 2. Of those that a mesh axis runs over, the one named last changes fastest.
Arguments:
- queries: bfloat16 [2, 8192, 2560], P('dp', 'ctx', 'head'), may hold values from -25 to 25
- keys: bfloat16 [2, 8192, 2560], P('dp', 'ctx', 'head'), may hold values from -25 to 25
- values: bfloat16 [2, 8192, 2560], P('dp', 'ctx', 'head'), may hold values from -6 to 6
- grad_y: bfloat16 [2, 8192, 2560], P('dp', 'ctx', 'head'), may hold values from -6 to 6
- out_gain: float32 [2560], P('head'), may hold values from 0.1 to 1.9
- offsets: int32 [2, 20], P(None, 'head'), may hold values from 0 to 63, as said below
Outputs:
- attended: bfloat16 [2, 8192, 2560], P('dp', 'ctx', 'head')
- query_grad: bfloat16 [2, 8192, 2560], P('dp', 'ctx', 'head')
- key_grad: bfloat16 [2, 8192, 2560], P('dp', 'ctx', 'head')
- value_grad: bfloat16 [2, 8192, 2560], P('dp', 'ctx', 'head')
- gain_grad: float32 [2560], P('head')
Inputs may be any that keep to these rules, and one draw needn't show every extreme that they name: Row 0 holds offsets below 8, row 1 offsets below 64.
All inputs are finite; a program needn't handle non-finite values.
Results may differ from a plain program's by a relative error of at most 0.011.
Values may be sent and summed in bfloat16 or wider, within the bound.
A program may use at most 64 MiB of HBM per device.

v0:
```python
import math
import jax
import jax.numpy as jnp
from jax import lax
from jax.sharding import PartitionSpec as P

HEAD_DIM = 128
SPAN = 4
R1 = 8
EPS = 1e-06


def group_gather(block, axis, group):
    count = lax.axis_size(axis)
    pieces = [block]
    for shift in range(1, group):
        route = []
        for src in range(count):
            base = src - src % group
            route.append((src, base + (src % group + shift) % group))
        pieces.append(lax.ppermute(block, axis, route))
    return jnp.concatenate(pieces, 0)


def pick_rows(source_rows, dilation, shifts):
    row_count, head_count, head_width = source_rows.shape
    grouped = source_rows.reshape(row_count // dilation, dilation, head_count, head_width)
    hit_mask = jnp.arange(dilation, dtype=jnp.int32).reshape(1, dilation, 1, 1) == shifts.reshape(
        1, 1, head_count, 1
    )
    chosen = jnp.where(hit_mask, grouped, jnp.zeros((), source_rows.dtype))
    return jnp.sum(chosen, axis=1, dtype=source_rows.dtype)


def place_rows(row_values, dilation, shifts):
    row_count, head_count, head_width = row_values.shape
    hit_mask = jnp.arange(dilation, dtype=jnp.int32).reshape(1, dilation, 1, 1) == shifts.reshape(
        1, 1, head_count, 1
    )
    spread = jnp.where(hit_mask, row_values[:, None], jnp.zeros((), row_values.dtype))
    return spread.reshape(row_count * dilation, head_count, head_width)


def level_scores(q_rows, k_rows):
    score_scale = 1.0 / math.sqrt(q_rows.shape[-1])
    return (
        jnp.einsum("qhe,khe->hqk", q_rows, k_rows, preferred_element_type=jnp.float32) * score_scale
    )


def attend(q_rows, k_rows, v_rows):
    scores = level_scores(q_rows, k_rows)
    row_max = jnp.max(scores, axis=-1, keepdims=True)
    log_total = row_max[..., 0] + jnp.log(jnp.sum(jnp.exp(scores - row_max), axis=-1))
    soft_rows = jnp.exp(scores - log_total[..., None]).astype(jnp.bfloat16)
    level_out = jnp.einsum("hqk,khe->qhe", soft_rows, v_rows, preferred_element_type=jnp.float32)
    return (level_out, log_total.T)


def score_grads(q_rows, k_rows, v_rows, log_total, grad_low, row_shift):
    score_scale = 1.0 / math.sqrt(q_rows.shape[-1])
    scores = level_scores(q_rows, k_rows)
    exact_soft = jnp.exp(scores - log_total.T[..., None])
    prob_grad = jnp.einsum("qhe,khe->hqk", grad_low, v_rows, preferred_element_type=jnp.float32)
    score_grad = (exact_soft * (prob_grad + row_shift.T[..., None]) * score_scale).astype(
        jnp.bfloat16
    )
    return (score_grad, exact_soft.astype(jnp.bfloat16))


def key_parts(score_grad, soft_low, q_rows, grad_low):
    k_part = jnp.einsum("hqk,qhe->khe", score_grad, q_rows, preferred_element_type=jnp.float32)
    v_part = jnp.einsum("hqk,qhe->khe", soft_low, grad_low, preferred_element_type=jnp.float32)
    return (k_part, v_part)


def query_part(score_grad, k_rows):
    return jnp.einsum("hqk,khe->qhe", score_grad, k_rows, preferred_element_type=jnp.float32)


def split_qkv(packed, head_count):
    width = head_count * HEAD_DIM
    shape = (packed.shape[0], head_count, HEAD_DIM)
    return tuple((packed[:, i * width : (i + 1) * width].reshape(shape) for i in range(3)))


def pack_grads(grad_low, row_shift):
    rows = grad_low.shape[0]
    return jnp.concatenate(
        [grad_low.astype(jnp.float32).reshape(rows, -1), row_shift.astype(jnp.float32)], 1
    )


def unpack_grads(packed, head_count):
    width = head_count * HEAD_DIM
    grad_low = packed[:, :width].astype(jnp.bfloat16).reshape(-1, head_count, HEAD_DIM)
    return (grad_low, packed[:, width:])


def shards(queries, keys, values, grad_y, out_gain, offsets):
    tokens = queries.shape[1]
    flat_width = queries.shape[2]
    head_count = flat_width // HEAD_DIM
    row_shape = (tokens, head_count, HEAD_DIM)
    q_own = queries[0].reshape(row_shape)
    k_own = keys[0].reshape(row_shape)
    v_own = values[0].reshape(row_shape)
    ctx_size = lax.axis_size("ctx")
    my_place = lax.axis_index("ctx")
    mid_shift = offsets[0]
    top_shift = offsets[1]
    positions = jnp.arange(tokens, dtype=jnp.int32)
    mid_hit = (positions % R1)[:, None] == mid_shift[None, :]
    top_hit = (positions % ctx_size)[:, None] == top_shift[None, :]
    mid_pack = jnp.concatenate(
        [pick_rows(x, R1, mid_shift).reshape(-1, flat_width) for x in (q_own, k_own, v_own)], 1
    )
    top_pack = jnp.concatenate(
        [pick_rows(x, ctx_size, top_shift).reshape(-1, flat_width) for x in (q_own, k_own, v_own)],
        1,
    )
    mid_rows = mid_pack.shape[0]
    top_rows = top_pack.shape[0]
    mid_all = group_gather(mid_pack, "ctx", SPAN)
    top_all = lax.all_gather(top_pack, "ctx", axis=0, tiled=True)
    mid_q, mid_k, mid_v = split_qkv(mid_all, head_count)
    top_q, top_k, top_v = split_qkv(top_all, head_count)
    top_start = my_place * top_rows
    base_out, base_total = attend(q_own, k_own, v_own)
    mid_out_all, mid_total_all = attend(mid_q, mid_k, mid_v)
    top_out_all, top_total_all = attend(top_q, top_k, top_v)
    mid_out = mid_out_all[:mid_rows]
    mid_total = mid_total_all[:mid_rows]
    top_out = lax.dynamic_slice_in_dim(top_out_all, top_start, top_rows, 0)
    top_total = lax.dynamic_slice_in_dim(top_total_all, top_start, top_rows, 0)
    mid_full = place_rows(mid_total[..., None], R1, mid_shift)[..., 0]
    top_full = place_rows(top_total[..., None], ctx_size, top_shift)[..., 0]
    row_max = jnp.maximum(base_total, jnp.where(mid_hit, mid_full, base_total))
    row_max = jnp.maximum(row_max, jnp.where(top_hit, top_full, base_total))
    base_expo = jnp.exp(base_total - row_max)
    mid_expo = jnp.where(mid_hit, jnp.exp(mid_full - row_max), 0.0)
    top_expo = jnp.where(top_hit, jnp.exp(top_full - row_max), 0.0)
    denom = base_expo + mid_expo + top_expo
    base_share = base_expo / denom
    mid_share = mid_expo / denom
    top_share = top_expo / denom
    attn = (
        base_share[..., None] * base_out
        + mid_share[..., None] * place_rows(mid_out, R1, mid_shift)
        + top_share[..., None] * place_rows(top_out, ctx_size, top_shift)
    )
    inv_rms = lax.rsqrt(jnp.mean(attn * attn, axis=-1, keepdims=True) + EPS)
    normed = attn * inv_rms
    gain_rows = out_gain.reshape(head_count, HEAD_DIM)
    attended = (normed * gain_rows).astype(jnp.bfloat16).reshape(1, tokens, flat_width)
    grad_full = grad_y[0].reshape(row_shape).astype(jnp.float32)
    gain_part = jnp.sum(grad_full * normed, axis=0).reshape(flat_width)
    gain_grad = lax.psum(gain_part, ("dp", "ctx"))
    grad_norm = grad_full * gain_rows
    grad_attn = inv_rms * (
        grad_norm - normed * jnp.mean(grad_norm * normed, axis=-1, keepdims=True)
    )
    inner = jnp.sum(grad_attn * attn, axis=-1)
    base_low = (base_share[..., None] * grad_attn).astype(jnp.bfloat16)
    base_shift = -(base_share * inner)
    base_grad, base_soft = score_grads(q_own, k_own, v_own, base_total, base_low, base_shift)
    base_dq = query_part(base_grad, k_own)
    base_dk, base_dv = key_parts(base_grad, base_soft, q_own, base_low)
    mid_sel = pick_rows(mid_share[..., None], R1, mid_shift)[..., 0]
    mid_low = (mid_sel[..., None] * pick_rows(grad_attn, R1, mid_shift)).astype(jnp.bfloat16)
    mid_row_shift = -(mid_sel * pick_rows(inner[..., None], R1, mid_shift)[..., 0])
    top_sel = pick_rows(top_share[..., None], ctx_size, top_shift)[..., 0]
    top_low = (top_sel[..., None] * pick_rows(grad_attn, ctx_size, top_shift)).astype(jnp.bfloat16)
    top_row_shift = -(top_sel * pick_rows(inner[..., None], ctx_size, top_shift)[..., 0])
    mid_low_all, mid_shift_all = unpack_grads(
        group_gather(pack_grads(mid_low, mid_row_shift), "ctx", SPAN), head_count
    )
    top_low_all, top_shift_all = unpack_grads(
        lax.all_gather(pack_grads(top_low, top_row_shift), "ctx", axis=0, tiled=True), head_count
    )
    mid_grad, mid_soft = score_grads(mid_q, mid_k, mid_v, mid_total_all, mid_low_all, mid_shift_all)
    mid_dq = query_part(mid_grad[:, :mid_rows], mid_k)
    mid_dk, mid_dv = key_parts(
        mid_grad[:, :, :mid_rows], mid_soft[:, :, :mid_rows], mid_q, mid_low_all
    )
    top_grad, top_soft = score_grads(top_q, top_k, top_v, top_total_all, top_low_all, top_shift_all)
    own_grad = lax.dynamic_slice_in_dim(top_grad, top_start, top_rows, 1)
    top_dq = query_part(own_grad, top_k)
    key_grad_cols = lax.dynamic_slice_in_dim(top_grad, top_start, top_rows, 2)
    key_soft_cols = lax.dynamic_slice_in_dim(top_soft, top_start, top_rows, 2)
    top_dk, top_dv = key_parts(key_grad_cols, key_soft_cols, top_q, top_low_all)
    query_grad = (
        base_dq + place_rows(mid_dq, R1, mid_shift) + place_rows(top_dq, ctx_size, top_shift)
    )
    key_grad = base_dk + place_rows(mid_dk, R1, mid_shift) + place_rows(top_dk, ctx_size, top_shift)
    value_grad = (
        base_dv + place_rows(mid_dv, R1, mid_shift) + place_rows(top_dv, ctx_size, top_shift)
    )
    out_shape = (1, tokens, flat_width)
    return (
        attended,
        query_grad.astype(jnp.bfloat16).reshape(out_shape),
        key_grad.astype(jnp.bfloat16).reshape(out_shape),
        value_grad.astype(jnp.bfloat16).reshape(out_shape),
        gain_grad,
    )


def solution(mesh):
    in_specs = (
        P("dp", "ctx", "head"),
        P("dp", "ctx", "head"),
        P("dp", "ctx", "head"),
        P("dp", "ctx", "head"),
        P("head"),
        P(None, "head"),
    )
    out_specs = (
        P("dp", "ctx", "head"),
        P("dp", "ctx", "head"),
        P("dp", "ctx", "head"),
        P("dp", "ctx", "head"),
        P("head"),
    )
    return jax.shard_map(shards, mesh=mesh, in_specs=in_specs, out_specs=out_specs, check_vma=False)
```

profile of v0, /device:TPU:256, one launch (start us, length us, event | category | flops | bytes accessed | tf_op | source)
XLA Modules:
  0.0 428.5 jit_solution(14037007713612233846)
XLA Ops:
  0.6 0.8 slice_bitcast_fusion.5
  1.4 0.6 copy-done.23
  2.0 1.5 fusion.24
  3.6 5.5 %collective-permute-start.2 = (bf16[16,1920]{1,0:T(8,128)(2,1)S(1)}, bf16[16,1920]{1,0:T(8,128)(2,1)S(1)}, u32[]{:S(2)}, u32[]{:S(2)}) collective-permute-start(bf16[16,1920]{1,0:T(8,128)(2,1)S(1)} %bitcast_dynamic-update-slice_fusion), channel_id=1, source_target_pairs={{0,12},{4,0},{8,4},{12,8},{16,28},{20,16},{24,20},{28,24},{32,44},... | collective-permute-start | bytes 184328 | tf_op jit(solution)/shard_map/ppermute | solution.py:21
  9.1 1.9 collective-permute-start.1
  11.0 2.9 collective-permute-start
  14.1 0.7 copy-done.1
  15.1 0.7 copy-done.2
  16.0 0.2 reshape_reshape_squeeze.21
  16.2 0.2 reshape_reshape_squeeze.22
  16.4 0.2 reshape_reshape_squeeze.23
  16.8 0.4 copy-done.21
  17.2 0.7 broadcast_in_dim.285
  17.9 0.6 broadcast_in_dim.278
  18.9 0.3 select_reduce_fusion.2
  19.2 50.0 %all-gather = bf16[64,2,1920]{2,1,0:T(2,128)(2,1)S(1)} all-gather(bf16[1,2,1920]{2,1,0:T(2,128)(2,1)S(1)} %maximum_bitcast_fusion.1), channel_id=1, replica_groups=mesh['dp'=2,'ctx'=64,'head'=4] {'ctx'}, dimensions={0}, use_global_device_ids=true | all-gather | bytes 499200 | tf_op jit(solution)/shard_map/all_gather | solution.py:125
  69.2 0.2 reshape.370
  69.9 0.3 fusion.67
  70.4 0.5 copy-done.7
  71.0 0.7 broadcast_in_dim.289
  71.7 0.3 fusion.70
  72.0 0.3 fusion.69
  72.5 0.2 fusion.68
  72.8 0.5 copy-done.9
  73.5 0.2 convolution_bitcast_fusion.4
  73.8 0.4 copy-done.19
  74.1 0.3 copy-done.18
  74.7 0.2 fusion.20
  74.9 0.5 multiply_reduce_fusion.3
  75.5 0.7 copy-done.13
  76.1 0.8 multiply_reduce_fusion
  76.9 0.7 copy-done.15
  77.6 0.3 fusion.19
  78.0 0.6 negate_bitcast_fusion
  79.1 0.6 pad_maximum_fusion.2
  79.7 2.6 collective-permute-start.5
  82.3 3.1 collective-permute-start.4
  85.4 2.3 collective-permute-start.3
  87.7 0.2 fusion.18
  88.0 0.4 copy-done.22
  88.7 49.2 %all-gather.1 = f32[64,2,645]{2,1,0:T(2,128)S(1)} all-gather(f32[1,2,645]{2,1,0:T(2,128)S(1)} %maximum_bitcast_fusion.2), channel_id=1, replica_groups=mesh['dp'=2,'ctx'=64,'head'=4] {'ctx'}, dimensions={0}, use_global_device_ids=true | all-gather | bytes 335400 | tf_op jit(solution)/shard_map/all_gather | solution.py:179
  137.9 0.3 reshape.372
  138.2 0.7 slice.99
  138.9 0.4 fusion.17
  139.3 0.5 copy-done.3
  140.0 0.2 convolution_bitcast_fusion.9
  140.1 0.5 copy-done.8
  140.7 0.3 fusion.16
  141.1 0.4 convolution_bitcast_fusion.8
  141.5 0.2 copy.319
  141.7 0.8 copy.357
  142.7 0.5 copy-done.17
  143.2 277.9 %psum.7 = f32[640]{0:T(1024)} all-reduce(f32[640]{0:T(1024)S(1)} %bitcast.273), channel_id=1, replica_groups=mesh['dp'=2,'ctx'=64,'head'=4] {'dp','ctx'}, use_global_device_ids=true, to_apply=%region_22.23 | all-reduce | flops 640 | bytes 5120 | tf_op jit(solution)/shard_map/psum | solution.py:158
  421.1 0.9 pad_maximum_fusion.1
  422.1 0.8 maximum_bitcast_fusion
  423.0 0.5 copy-done.10
  423.9 0.2 convolution_bitcast_fusion.7
  424.1 0.6 copy-done.12
  424.7 0.2 fusion.14
  425.1 0.8 copy.359
  426.0 0.3 fusion.13
  426.4 0.8 copy.358
  427.2 0.3 fusion.15
  427.7 0.8 copy.360
  (112 shorter events, 5.3 us)
Async XLA Ops:
  1.4 0.6 copy-start.23
  1.4 15.2 %copy-start.25 = (s32[5]{0:T(128)}, s32[5]{0:T(128)S(1)}, u32[]{:S(2)}) copy-start(s32[5]{0:T(128)S(1)} %get-tuple-element.62) | copy-start | bytes 64
  2.0 15.9 %copy-start.14 = (pred[8,5]{0,1:T(8,128)(4,1)}, pred[8,5]{0,1:T(8,128)(4,1)S(1)}, u32[]{:S(2)}) copy-start(pred[8,5]{0,1:T(8,128)(4,1)S(1)} %iota_compare_fusion.1) | copy-start | bytes 124
  2.0 11.9 %copy-start = (bf16[1,128,640]{2,1,0:T(8,128)(2,1)S(1)}, bf16[1,128,640]{2,1,0:T(8,128)(2,1)}, u32[]{:S(2)}) copy-start(bf16[1,128,640]{2,1,0:T(8,128)(2,1)} %param.6) | copy-start | bytes 491524
  3.6 68.8 %collective-permute-start.2 = (bf16[16,1920]{1,0:T(8,128)(2,1)S(1)}, bf16[16,1920]{1,0:T(8,128)(2,1)S(1)}, u32[]{:S(2)}, u32[]{:S(2)}) collective-permute-start(bf16[16,1920]{1,0:T(8,128)(2,1)S(1)} %bitcast_dynamic-update-slice_fusion), channel_id=1, source_target_pairs={{0,12},{4,0},{8,4},{12,8},{16,28},{20,16},{24,20},{28,24},{32,44},... | collective-permute-start | bytes 184328 | tf_op jit(solution)/shard_map/ppermute | solution.py:21
  9.1 63.3 %collective-permute-start.1 = (bf16[16,1920]{1,0:T(8,128)(2,1)S(1)}, bf16[16,1920]{1,0:T(8,128)(2,1)S(1)}, u32[]{:S(2)}, u32[]{:S(2)}) collective-permute-start(bf16[16,1920]{1,0:T(8,128)(2,1)S(1)} %bitcast_dynamic-update-slice_fusion), channel_id=1, source_target_pairs={{0,8},{4,12},{8,0},{12,4},{16,24},{20,28},{24,16},{28,20},{32,40},... | collective-permute-start | bytes 184328 | tf_op jit(solution)/shard_map/ppermute | solution.py:21
  11.0 61.3 %collective-permute-start = (bf16[16,1920]{1,0:T(8,128)(2,1)S(1)}, bf16[16,1920]{1,0:T(8,128)(2,1)S(1)}, u32[]{:S(2)}, u32[]{:S(2)}) collective-permute-start(bf16[16,1920]{1,0:T(8,128)(2,1)S(1)} %bitcast_dynamic-update-slice_fusion), channel_id=1, source_target_pairs={{0,4},{4,8},{8,12},{12,0},{16,20},{20,24},{24,28},{28,16},{32,36},... | collective-permute-start | bytes 184328 | tf_op jit(solution)/shard_map/ppermute | solution.py:21
  14.0 0.9 copy-start.1
  14.9 0.9 copy-start.2
  16.4 2.2 copy-start.6
  16.7 0.5 copy-start.21
  70.3 0.6 copy-start.7
  72.4 1.0 copy-start.4
  72.7 0.6 copy-start.9
  73.5 0.7 copy-start.19
  73.5 0.7 copy-start.26
  73.7 0.7 copy-start.18
  73.7 0.7 copy-start.11
  73.8 0.7 copy-start.24
  75.4 0.7 copy-start.13
  76.9 0.7 copy-start.15
  79.7 341.3 %collective-permute-start.5 = (f32[16,645]{1,0:T(8,128)}, f32[16,645]{1,0:T(8,128)}, u32[]{:S(2)}, u32[]{:S(2)}) collective-permute-start(f32[16,645]{1,0:T(8,128)} %pad_maximum_fusion.2), channel_id=1, source_target_pairs={{0,12},{4,0},{8,4},{12,8},{16,28},{20,16},{24,20},{28,24},{32,44},... | collective-permute-start | bytes 123848 | tf_op jit(solution)/shard_map/ppermute | solution.py:21
  82.3 338.8 %collective-permute-start.4 = (f32[16,645]{1,0:T(8,128)}, f32[16,645]{1,0:T(8,128)}, u32[]{:S(2)}, u32[]{:S(2)}) collective-permute-start(f32[16,645]{1,0:T(8,128)} %pad_maximum_fusion.2), channel_id=1, source_target_pairs={{0,8},{4,12},{8,0},{12,4},{16,24},{20,28},{24,16},{28,20},{32,40},... | collective-permute-start | bytes 123848 | tf_op jit(solution)/shard_map/ppermute | solution.py:21
  85.4 335.7 %collective-permute-start.3 = (f32[16,645]{1,0:T(8,128)}, f32[16,645]{1,0:T(8,128)}, u32[]{:S(2)}, u32[]{:S(2)}) collective-permute-start(f32[16,645]{1,0:T(8,128)} %pad_maximum_fusion.2), channel_id=1, source_target_pairs={{0,4},{4,8},{8,12},{12,0},{16,20},{20,24},{24,28},{28,16},{32,36},... | collective-permute-start | bytes 123848 | tf_op jit(solution)/shard_map/ppermute | solution.py:21
  87.7 0.6 copy-start.22
  138.2 0.7 copy-start.16
  138.9 0.9 copy-start.3
  140.0 0.7 copy-start.8
  141.7 0.8 copy-start.20
  142.5 0.7 copy-start.17
  422.1 0.9 copy-start.5
  422.8 0.7 copy-start.10
  424.1 0.6 copy-start.12
where the time goes:
time: 429 us
  blocking collectives  377 us (88%)
  local copies, waits for them, and re-layouts  19.9 us (5%)
  starting transfers between devices  18.3 us (4%)
  other arithmetic  7.42 us (2%)
  matrix products  4.56 us (1%)
    psum x1, blocking collectives, shards(): gain_grad = lax.psum(gain_part, ('dp', 'ctx'))  278 us
    all_gather x1, blocking collectives, shards(): top_all = lax.all_gather(top_pack, 'ctx', axis=0, tiled=True)  50 us
    all_gather x1, blocking collectives, shards(): lax.all_gather(pack_grads(top_low, top_row_shift), 'ctx', axis=0, tiled=T...  49.2 us
    ppermute x6, starting transfers between devices, group_gather(): pieces.append(lax.ppermute(block, axis, route))  18.3 us
    unnamed x69, local copies, waits for them, and re-layouts  13.1 us
  transfers between devices with their start and end apart: 6, of which 0 were waited for; matrix products, arithmetic and copies ran while one was open for 2% of the time, Pallas kernels for 0%

commit v1 on v0

--- a/solution.py
+++ b/solution.py
@@ -155,7 +155,7 @@
     attended = (normed * gain_rows).astype(jnp.bfloat16).reshape(1, tokens, flat_width)
     grad_full = grad_y[0].reshape(row_shape).astype(jnp.float32)
     gain_part = jnp.sum(grad_full * normed, axis=0).reshape(flat_width)
-    gain_grad = lax.psum(gain_part, ("dp", "ctx"))
+    gain_grad = lax.psum(lax.psum(gain_part, "ctx"), "dp")
     grad_norm = grad_full * gain_rows
     grad_attn = inv_rms * (
         grad_norm - normed * jnp.mean(grad_norm * normed, axis=-1, keepdims=True)

time: 429 us -> 304 us (0.71)
  the two profiles are of different devices: /device:TPU:256 before, /device:TPU:1 now
where the time goes in v1:
time: 304 us; the launch traced here: 303 us
  blocking collectives  251 us (83%)
  local copies, waits for them, and re-layouts  19.9 us (7%)
  starting transfers between devices  19 us (6%)
  other arithmetic  7.42 us (2%)
  matrix products  4.56 us (1%)
    psum x2, blocking collectives, shards(): gain_grad = lax.psum(lax.psum(gain_part, 'ctx'), 'dp')  169 us
    all_gather x1, blocking collectives, shards(): top_all = lax.all_gather(top_pack, 'ctx', axis=0, tiled=True)  44.2 us
    all_gather x1, blocking collectives, shards(): lax.all_gather(pack_grads(top_low, top_row_shift), 'ctx', axis=0, tiled=T...  37.9 us
    ppermute x6, starting transfers between devices, group_gather(): pieces.append(lax.ppermute(block, axis, route))  19 us
    unnamed x69, local copies, waits for them, and re-layouts  13.1 us
  transfers between devices with their start and end apart: 6, of which 0 were waited for; matrix products, arithmetic and copies ran while one was open for 3% of the time, Pallas kernels for 0%

profile of v1, /device:TPU:1, one launch (start us, length us, event | category | flops | bytes accessed | tf_op | source)
XLA Modules:
  0.0 303.0 jit_solution(10014502177558052411)
XLA Ops:
  0.6 0.8 slice_bitcast_fusion.5
  1.4 0.6 copy-done.23
  2.0 1.5 fusion.24
  3.6 6.1 %collective-permute-start.2 = (bf16[16,1920]{1,0:T(8,128)(2,1)S(1)}, bf16[16,1920]{1,0:T(8,128)(2,1)S(1)}, u32[]{:S(2)}, u32[]{:S(2)}) collective-permute-start(bf16[16,1920]{1,0:T(8,128)(2,1)S(1)} %bitcast_dynamic-update-slice_fusion), channel_id=1, source_target_pairs={{0,12},{4,0},{8,4},{12,8},{16,28},{20,16},{24,20},{28,24},{32,44},... | collective-permute-start | bytes 184328 | tf_op jit(solution)/shard_map/ppermute | solution.py:21
  9.7 1.9 collective-permute-start.1
  11.6 2.3 collective-permute-start
  14.1 0.7 copy-done.1
  15.0 0.7 copy-done.2
  16.0 0.2 reshape_reshape_squeeze.21
  16.2 0.2 reshape_reshape_squeeze.22
  16.4 0.2 reshape_reshape_squeeze.23
  16.8 0.4 copy-done.21
  17.2 0.7 broadcast_in_dim.285
  17.9 0.6 broadcast_in_dim.278
  18.9 0.3 select_reduce_fusion.2
  19.2 44.2 %all-gather = bf16[64,2,1920]{2,1,0:T(2,128)(2,1)S(1)} all-gather(bf16[1,2,1920]{2,1,0:T(2,128)(2,1)S(1)} %maximum_bitcast_fusion.1), channel_id=1, replica_groups=mesh['dp'=2,'ctx'=64,'head'=4] {'ctx'}, dimensions={0}, use_global_device_ids=true | all-gather | bytes 499200 | tf_op jit(solution)/shard_map/all_gather | solution.py:125
  63.4 0.2 reshape.370
  64.1 0.3 fusion.67
  64.5 0.5 copy-done.7
  65.2 0.7 broadcast_in_dim.289
  65.9 0.3 fusion.70
  66.2 0.3 fusion.69
  66.6 0.2 fusion.68
  66.9 0.5 copy-done.9
  67.7 0.2 convolution_bitcast_fusion.4
  67.9 0.4 copy-done.19
  68.3 0.3 copy-done.18
  68.9 0.2 fusion.20
  69.1 0.5 multiply_reduce_fusion.3
  69.6 0.7 copy-done.13
  70.3 0.8 multiply_reduce_fusion
  71.1 0.7 copy-done.15
  71.8 0.3 fusion.19
  72.2 0.6 negate_bitcast_fusion
  73.2 0.6 pad_maximum_fusion.2
  73.9 3.9 %collective-permute-start.5 = (f32[16,645]{1,0:T(8,128)}, f32[16,645]{1,0:T(8,128)}, u32[]{:S(2)}, u32[]{:S(2)}) collective-permute-start(f32[16,645]{1,0:T(8,128)} %pad_maximum_fusion.2), channel_id=1, source_target_pairs={{0,12},{4,0},{8,4},{12,8},{16,28},{20,16},{24,20},{28,24},{32,44},... | collective-permute-start | bytes 123848 | tf_op jit(solution)/shard_map/ppermute | solution.py:21
  77.8 2.8 collective-permute-start.4
  80.6 1.9 collective-permute-start.3
  82.5 0.2 fusion.18
  82.8 0.4 copy-done.22
  83.5 37.9 %all-gather.1 = f32[64,2,645]{2,1,0:T(2,128)S(1)} all-gather(f32[1,2,645]{2,1,0:T(2,128)S(1)} %maximum_bitcast_fusion.2), channel_id=1, replica_groups=mesh['dp'=2,'ctx'=64,'head'=4] {'ctx'}, dimensions={0}, use_global_device_ids=true | all-gather | bytes 335400 | tf_op jit(solution)/shard_map/all_gather | solution.py:179
  121.4 0.3 reshape.372
  121.7 0.7 slice.99
  122.4 0.4 fusion.17
  122.8 0.5 copy-done.3
  123.7 0.5 copy-done.8
  124.2 0.3 fusion.16
  124.6 0.4 convolution_bitcast_fusion.8
  125.0 0.2 copy.319
  125.2 0.8 copy.357
  126.2 0.5 copy-done.17
  126.7 113.0 %psum.14 = f32[640]{0:T(1024)S(1)} all-reduce(f32[640]{0:T(1024)S(1)} %bitcast.273), channel_id=1, replica_groups=mesh['dp'=2,'ctx'=64,'head'=4] {'ctx'}, use_global_device_ids=true, to_apply=%region_22.23 | all-reduce | flops 640 | bytes 5120 | tf_op jit(solution)/shard_map/psum | solution.py:158
  239.7 55.9 %psum.15 = f32[640]{0:T(1024)} all-reduce(f32[640]{0:T(1024)S(1)} %psum.14), channel_id=1, replica_groups=mesh['dp'=2,'ctx'=64,'head'=4] {'dp'}, use_global_device_ids=true, to_apply=%region_23.24 | all-reduce | flops 640 | bytes 5120 | tf_op jit(solution)/shard_map/psum | solution.py:158
  295.6 0.9 pad_maximum_fusion.1
  296.6 0.8 maximum_bitcast_fusion
  297.5 0.5 copy-done.10
  298.4 0.2 convolution_bitcast_fusion.7
  298.6 0.6 copy-done.12
  299.2 0.2 fusion.14
  299.7 0.8 copy.359
  300.5 0.3 fusion.13
  300.9 0.8 copy.358
  301.7 0.3 fusion.15
  302.2 0.8 copy.360
  (113 shorter events, 5.5 us)
Async XLA Ops:
  1.4 0.6 copy-start.23
  1.4 15.2 %copy-start.25 = (s32[5]{0:T(128)}, s32[5]{0:T(128)S(1)}, u32[]{:S(2)}) copy-start(s32[5]{0:T(128)S(1)} %get-tuple-element.62) | copy-start | bytes 64
  2.0 15.9 %copy-start.14 = (pred[8,5]{0,1:T(8,128)(4,1)}, pred[8,5]{0,1:T(8,128)(4,1)S(1)}, u32[]{:S(2)}) copy-start(pred[8,5]{0,1:T(8,128)(4,1)S(1)} %iota_compare_fusion.1) | copy-start | bytes 124
  2.0 11.9 %copy-start = (bf16[1,128,640]{2,1,0:T(8,128)(2,1)S(1)}, bf16[1,128,640]{2,1,0:T(8,128)(2,1)}, u32[]{:S(2)}) copy-start(bf16[1,128,640]{2,1,0:T(8,128)(2,1)} %param.6) | copy-start | bytes 491524
  3.6 62.9 %collective-permute-start.2 = (bf16[16,1920]{1,0:T(8,128)(2,1)S(1)}, bf16[16,1920]{1,0:T(8,128)(2,1)S(1)}, u32[]{:S(2)}, u32[]{:S(2)}) collective-permute-start(bf16[16,1920]{1,0:T(8,128)(2,1)S(1)} %bitcast_dynamic-update-slice_fusion), channel_id=1, source_target_pairs={{0,12},{4,0},{8,4},{12,8},{16,28},{20,16},{24,20},{28,24},{32,44},... | collective-permute-start | bytes 184328 | tf_op jit(solution)/shard_map/ppermute | solution.py:21
  9.7 56.9 %collective-permute-start.1 = (bf16[16,1920]{1,0:T(8,128)(2,1)S(1)}, bf16[16,1920]{1,0:T(8,128)(2,1)S(1)}, u32[]{:S(2)}, u32[]{:S(2)}) collective-permute-start(bf16[16,1920]{1,0:T(8,128)(2,1)S(1)} %bitcast_dynamic-update-slice_fusion), channel_id=1, source_target_pairs={{0,8},{4,12},{8,0},{12,4},{16,24},{20,28},{24,16},{28,20},{32,40},... | collective-permute-start | bytes 184328 | tf_op jit(solution)/shard_map/ppermute | solution.py:21
  11.6 55.0 %collective-permute-start = (bf16[16,1920]{1,0:T(8,128)(2,1)S(1)}, bf16[16,1920]{1,0:T(8,128)(2,1)S(1)}, u32[]{:S(2)}, u32[]{:S(2)}) collective-permute-start(bf16[16,1920]{1,0:T(8,128)(2,1)S(1)} %bitcast_dynamic-update-slice_fusion), channel_id=1, source_target_pairs={{0,4},{4,8},{8,12},{12,0},{16,20},{20,24},{24,28},{28,16},{32,36},... | collective-permute-start | bytes 184328 | tf_op jit(solution)/shard_map/ppermute | solution.py:21
  14.0 0.9 copy-start.1
  14.9 0.9 copy-start.2
  16.4 2.2 copy-start.6
  16.7 0.5 copy-start.21
  64.5 0.6 copy-start.7
  66.6 1.0 copy-start.4
  66.9 0.6 copy-start.9
  67.6 0.7 copy-start.19
  67.7 0.7 copy-start.26
  67.9 0.7 copy-start.18
  67.9 0.7 copy-start.11
  67.9 0.7 copy-start.24
  69.6 0.7 copy-start.13
  71.1 0.7 copy-start.15
  73.9 221.7 %collective-permute-start.5 = (f32[16,645]{1,0:T(8,128)}, f32[16,645]{1,0:T(8,128)}, u32[]{:S(2)}, u32[]{:S(2)}) collective-permute-start(f32[16,645]{1,0:T(8,128)} %pad_maximum_fusion.2), channel_id=1, source_target_pairs={{0,12},{4,0},{8,4},{12,8},{16,28},{20,16},{24,20},{28,24},{32,44},... | collective-permute-start | bytes 123848 | tf_op jit(solution)/shard_map/ppermute | solution.py:21
  77.8 217.8 %collective-permute-start.4 = (f32[16,645]{1,0:T(8,128)}, f32[16,645]{1,0:T(8,128)}, u32[]{:S(2)}, u32[]{:S(2)}) collective-permute-start(f32[16,645]{1,0:T(8,128)} %pad_maximum_fusion.2), channel_id=1, source_target_pairs={{0,8},{4,12},{8,0},{12,4},{16,24},{20,28},{24,16},{28,20},{32,40},... | collective-permute-start | bytes 123848 | tf_op jit(solution)/shard_map/ppermute | solution.py:21
  80.6 215.0 %collective-permute-start.3 = (f32[16,645]{1,0:T(8,128)}, f32[16,645]{1,0:T(8,128)}, u32[]{:S(2)}, u32[]{:S(2)}) collective-permute-start(f32[16,645]{1,0:T(8,128)} %pad_maximum_fusion.2), channel_id=1, source_target_pairs={{0,4},{4,8},{8,12},{12,0},{16,20},{20,24},{24,28},{28,16},{32,36},... | collective-permute-start | bytes 123848 | tf_op jit(solution)/shard_map/ppermute | solution.py:21
  82.5 0.6 copy-start.22
  121.7 0.7 copy-start.16
  122.4 0.9 copy-start.3
  123.5 0.7 copy-start.8
  125.2 0.8 copy-start.20
  126.0 0.7 copy-start.17
  296.6 0.9 copy-start.5
  297.4 0.7 copy-start.10
  298.6 0.6 copy-start.12
